TPU v7x, 512 devices: a whole 4x4x16 slice. The times are simulated.
512 devices in a mesh: term: 8 (over y, core), doc: 16 (over z), enc: 4 (over x).
Axes of the slice: x: 4, y: 4, z: 16, core: 2. Of those that a mesh axis runs over, the one named last changes fastest.
Arguments:
- query_weights: bfloat16 [1024, 30720], P('enc', ('term', 'doc')), may hold values from 0.049804688 to 2
- tile_terms: int32 [30720], P(('term', 'doc')), may hold values from 0 to 59
- tile_blocks: int32 [30720], P(('term', 'doc')), may hold values from 0 to 15
- tile_counts: int32 [128], P(('term', 'doc')), may hold values from 60 to 240, as said below
- impacts: bfloat16 [30720, 64, 128], P(('term', 'doc')), may hold values from -0.015625 to 0.015625
Outputs:
- scores: float32 [2048, 1024], P('doc', 'enc')
Inputs may be any that keep to these rules, and one draw needn't show every extreme that they name: Slots at positions tile_counts or later of a device's list are padding and contribute nothing; some device has all 240 slots live.
All inputs are finite; a program needn't handle non-finite values.
Results may differ from a plain program's by a relative error of at most 0.0003.
Values may be sent and summed in bfloat16 or wider, within the bound.
No kernel may reach another device: no remote copies, remote signals or barrier semaphores. Data moves between devices by JAX's collectives and lax.ppermute only.
A program may use at most 64 MiB of HBM per device.

v0:
```python
import jax
import jax.numpy as jnp
from jax import lax
from jax.sharding import PartitionSpec as P


def block_size(tiles):
    largest = 1
    for divisor in range(1, 65):
        if tiles % divisor == 0:
            largest = divisor
    return largest


def per_device(query_weights, tile_terms, tile_blocks, tile_counts, impacts):
    range_rows = lax.all_gather(query_weights, "doc", axis=1, tiled=True)
    queries = range_rows.shape[0]
    tiles, term_block, doc_block = impacts.shape
    owners = lax.axis_size("doc")
    grouped = range_rows.reshape(queries, range_rows.shape[1] // term_block, term_block)
    step = block_size(tiles)
    live = jnp.arange(tiles, dtype=jnp.int32) < tile_counts[0]
    owner_ids = jnp.arange(owners, dtype=jnp.int32)

    def accumulate(total, number):
        start = number * step
        term_now = lax.dynamic_slice_in_dim(tile_terms, start, step)
        owner_now = lax.dynamic_slice_in_dim(tile_blocks, start, step)
        keep_now = lax.dynamic_slice_in_dim(live, start, step)
        tile_now = lax.dynamic_slice_in_dim(impacts, start, step)
        picked = jnp.take(grouped, term_now, axis=1)
        product = jnp.einsum("qnk,nkd->ndq", picked, tile_now, preferred_element_type=jnp.float32)
        select = ((owner_now[:, None] == owner_ids[None, :]) & keep_now[:, None]).astype(
            jnp.float32
        )
        added = jnp.einsum("ndq,nb->bdq", product, select, precision=lax.Precision.HIGHEST)
        return (total + added, None)

    start_total = jnp.zeros((owners, doc_block, queries), jnp.float32)
    total, unused = lax.scan(accumulate, start_total, jnp.arange(tiles // step, dtype=jnp.int32))
    partial_value = total.reshape(owners * doc_block, queries)
    mine = lax.psum_scatter(partial_value, "doc", scatter_dimension=0, tiled=True)
    scores = lax.psum(mine, "term")
    return scores


def solution(mesh):
    return jax.shard_map(
        per_device,
        mesh=mesh,
        in_specs=(
            P("enc", ("term", "doc")),
            P(("term", "doc")),
            P(("term", "doc")),
            P(("term", "doc")),
            P(("term", "doc"), None, None),
        ),
        out_specs=P("doc", "enc"),
        check_vma=False,
    )
```

profile of v0, /device:TPU:2, one launch (start us, length us, event | category | flops | bytes accessed | tf_op | source)
XLA Modules:
  0.0 312.8 jit_solution(1491762189442942286)
XLA Ops:
  6.5 0.0 all-gather.2.cloned.1.call-start
  6.5 0.7 all-gather.2.cloned.1.call-update
  7.3 0.0 reduce-scatter.2.cloned.1.call-start
  8.0 78.3 %all-gather.2.cloned.1.call-done = bf16[256,3840]{0,1:T(8,128)(2,1)} async-done(((bf16[256,240]{0,1:T(8,128)(2,1)}), bf16[256,3840]{0,1:T(8,128)(2,1)}) %all-gather.2.cloned.1.call-update) | async-done | bytes 1966096 | tf_op jit(solution)/shard_map/all_gather | solution.py:16
  86.2 67.8 %while.11 = (s32[]{:T(128)}, f32[16,128,256]{2,0,1:T(8,128)}, s32[4]{0:T(128)S(1)}, s32[240]{0:T(256)}, pred[240]{0:T(512)(128)(4,1)S(1)}, /*index=5*/bf16[240,6...) while((s32[]{:T(128)}, f32[16,128,256]{2,0,1:T(8,128)}, ...), condition=%wide.region_1.2_spmd.clone, body=%wide.region_0.1_spmd.clone.sunk | while | flops 631180544 | bytes 43587780 | solution.py:40
  86.2 0.6 dynamic_slice.30
  87.5 0.1 dynamic_slice.32
  87.6 0.8 dynamic_slice.31
  88.3 0.8 compare_and_fusion.2
  89.1 2.2 gather_fusion
  91.3 2.6 fusion.28
  93.9 7.9 %select_add_fusion.2 = f32[16,128,256]{2,0,1:T(8,128)S(1)} fusion(f32[16,128,256]{2,0,1:T(8,128)S(1)} %copy-done, f32[60,128,256]{2,1,0:T(8,128)S(1)} %fusion.28, pred[]{:T(512)S(6)} %compare.3, s32[60]{0:T(128)S(1)} %dynamic_slice.31, pred[60]{0:T(512)(128)(4,1)S(1)} %dynamic_slice.32), kind=kOutput, calls=%fused_computation.4.clone.1 | convolution fusion | flops 378537856 | bytes 12058925 | tf_op jit(solution)/shard_map/while/body/eval_jaxpr/ndq,nb->bdq/dot_general | solution.py:36
  101.9 1.3 copy-done.1
  103.2 0.6 dynamic_slice.30
  104.4 0.1 dynamic_slice.32
  104.5 0.8 dynamic_slice.31
  105.2 0.8 compare_and_fusion.2
  106.0 2.2 gather_fusion
  108.3 2.6 fusion.28
  110.9 0.0 copy-done
  110.9 7.9 %select_add_fusion.2 = f32[16,128,256]{2,0,1:T(8,128)S(1)} fusion(f32[16,128,256]{2,0,1:T(8,128)S(1)} %copy-done, f32[60,128,256]{2,1,0:T(8,128)S(1)} %fusion.28, pred[]{:T(512)S(6)} %compare.3, s32[60]{0:T(128)S(1)} %dynamic_slice.31, pred[60]{0:T(512)(128)(4,1)S(1)} %dynamic_slice.32), kind=kOutput, calls=%fused_computation.4.clone.1 | convolution fusion | flops 378537856 | bytes 12058925 | tf_op jit(solution)/shard_map/while/body/eval_jaxpr/ndq,nb->bdq/dot_general | solution.py:36
  118.8 0.0 copy-start.1
  118.8 1.3 copy-done.1
  120.1 0.6 dynamic_slice.30
  121.4 0.1 dynamic_slice.32
  121.4 0.8 dynamic_slice.31
  122.2 0.8 compare_and_fusion.2
  122.9 2.2 gather_fusion
  125.2 0.0 copy-start
  125.2 2.6 fusion.28
  127.8 7.9 %select_add_fusion.2 = f32[16,128,256]{2,0,1:T(8,128)S(1)} fusion(f32[16,128,256]{2,0,1:T(8,128)S(1)} %copy-done, f32[60,128,256]{2,1,0:T(8,128)S(1)} %fusion.28, pred[]{:T(512)S(6)} %compare.3, s32[60]{0:T(128)S(1)} %dynamic_slice.31, pred[60]{0:T(512)(128)(4,1)S(1)} %dynamic_slice.32), kind=kOutput, calls=%fused_computation.4.clone.1 | convolution fusion | flops 378537856 | bytes 12058925 | tf_op jit(solution)/shard_map/while/body/eval_jaxpr/ndq,nb->bdq/dot_general | solution.py:36
  135.7 1.3 copy-done.1
  137.1 0.6 dynamic_slice.30
  138.3 0.1 dynamic_slice.32
  138.4 0.8 dynamic_slice.31
  139.1 0.8 compare_and_fusion.2
  139.9 2.2 gather_fusion
  142.1 2.6 fusion.28
  144.8 7.9 %select_add_fusion.2 = f32[16,128,256]{2,0,1:T(8,128)S(1)} fusion(f32[16,128,256]{2,0,1:T(8,128)S(1)} %copy-done, f32[60,128,256]{2,1,0:T(8,128)S(1)} %fusion.28, pred[]{:T(512)S(6)} %compare.3, s32[60]{0:T(128)S(1)} %dynamic_slice.31, pred[60]{0:T(512)(128)(4,1)S(1)} %dynamic_slice.32), kind=kOutput, calls=%fused_computation.4.clone.1 | convolution fusion | flops 378537856 | bytes 12058925 | tf_op jit(solution)/shard_map/while/body/eval_jaxpr/ndq,nb->bdq/dot_general | solution.py:36
  152.7 0.0 copy-start.1
  152.7 1.3 copy-done.1
  154.0 4.1 %copy.8 = f32[16,128,256]{2,1,0:T(8,128)} copy(f32[16,128,256]{2,0,1:T(8,128)} %get-tuple-element.52) | data formatting | bytes 4194304 | tf_op jit(solution)/shard_map/while | solution.py:40
  158.1 0.0 reduce-scatter.2.cloned.1.call-update
  158.2 0.0 all-reduce.2.cloned.1.call-start
  158.2 71.0 %reduce-scatter.2.cloned.1.call-done = f32[128,256]{1,0:T(8,128)} async-done(((f32[2048,256]{1,0:T(8,128)}), f32[128,256]{1,0:T(8,128)}) %reduce-scatter.2.cloned.1.call-update) | async-done | bytes 131088 | tf_op jit(solution)/shard_map/reduce_scatter | solution.py:42
  229.3 0.0 all-reduce.2.cloned.1.call-update
  229.3 75.4 %all-reduce.2.cloned.1.call-done = f32[128,256]{1,0:T(8,128)} async-done(((f32[128,256]{1,0:T(8,128)}), f32[128,256]{1,0:T(8,128)}) %all-reduce.2.cloned.1.call-update) | async-done | bytes 131088 | tf_op jit(solution)/shard_map/psum | solution.py:43
  304.7 1.6 copy.24
  (15 shorter events, 0.0 us)
Async XLA Ops:
  6.5 79.7 %all-gather.2.cloned.1.call-start = ((), (), s32[]{:S(2)}) async-start(), calls=%async_computation.1 | async-start | bytes 2088960 | tf_op jit(solution)/shard_map/all_gather | solution.py:16
  7.3 222.0 %reduce-scatter.2.cloned.1.call-start = ((), (), s32[]{:S(2)}) async-start(), calls=%async_computation.2 | async-start | bytes 2228224 | tf_op jit(solution)/shard_map/reduce_scatter | solution.py:42
  91.3 2.6 copy-start
  101.8 1.3 copy-start.1
  108.2 2.6 copy-start
  118.8 1.3 copy-start.1
  125.2 2.6 copy-start
  135.7 1.3 copy-start.1
  142.1 2.6 copy-start
  152.7 1.3 copy-start.1
  158.2 146.6 %all-reduce.2.cloned.1.call-start = ((), (), s32[]{:S(2)}) async-start(), calls=%async_computation.3 | async-start | bytes 262144 | tf_op jit(solution)/shard_map/psum | solution.py:43
Sparse Core Ops, SparseCore 0:
  9.4 76.7 all-gather.1
  158.3 70.9 reduce-scatter.1
  231.6 73.0 all-reduce.1
where the time goes:
time: 313 us
  waiting for transfers between devices  225 us (72%)
  matrix products  42 us (13%)
  local copies, waits for them, and re-layouts  25.7 us (8%)
  between operations  13.8 us (4%)
    all_gather x1, waiting for transfers between devices, per_device(): range_rows = lax.all_gather(query_weights, 'doc', axis=1, tiled=True)  78.3 us
    psum x1, waiting for transfers between devices, per_device(): scores = lax.psum(mine, 'term')  75.4 us
    reduce_scatter x1, waiting for transfers between devices, per_device(): lax.psum_scatter(partial_value, 'doc', scatter_dimension=0, tiled=True)  71 us
    dot_general x4, matrix products, accumulate(): jnp.einsum('ndq,nb->bdq', product, select, precision=lax.Precision.HIGHEST)  31.6 us
    dot_general x4, matrix products, accumulate(): jnp.einsum('qnk,nkd->ndq', picked, tile_now, preferred_element_type=jnp.f...  10.5 us
    gather x4, local copies, waits for them, and re-layouts, accumulate(): picked = jnp.take(grouped, term_now, axis=1)  8.92 us
  transfers between devices with their start and end apart: 3, of which 3 were waited for; matrix products, arithmetic and copies ran while one was open for 0% of the time, Pallas kernels for 0%

commit v1 on v0

--- a/solution.py
+++ b/solution.py
@@ -1,7 +1,39 @@
+import functools
 import jax
 import jax.numpy as jnp
 from jax import lax
 from jax.sharding import PartitionSpec as P
+
+
+def attach_meshes(row_data, dim_k):
+    row_data = jnp.moveaxis(row_data, 0, dim_k)
+    high = row_data.shape
+    z2 = row_data.reshape(*high[:dim_k], high[dim_k] * high[dim_k + 1], *high[dim_k + 2 :])
+    return z2
+
+
+def finish_local_data_up(z_in, row_axis, row_dim):
+    chips = lax.axis_size(row_axis)
+    wide_out = range(chips)
+    r_now = map(lambda dev_i: (dev_i, (dev_i + 1) % chips), wide_out)
+    shelf = list(r_now)
+    p_next, y1 = ([], [])
+    k = 0
+    in_order = [(rr, no) for no, rr in shelf]
+    while k < chips - 1:
+        if k % 2 == 0:
+            p_next.append(lax.ppermute(p_next[-1] if p_next else z_in, row_axis, shelf))
+        else:
+            y1.append(lax.ppermute(y1[-1] if y1 else z_in, row_axis, in_order))
+        k += 1
+    near = jnp.stack([*p_next[::-1], z_in, *y1], axis=0)
+    y = lax.axis_index(row_axis) - len(p_next)
+    near = near[(jnp.arange(chips) - y) % chips]
+    even = attach_meshes(near, row_dim)
+    return even
+
+
+post_state = functools.partial(finish_local_data_up, row_axis="doc", row_dim=1)
 
 
 def block_size(tiles):
@@ -13,7 +45,7 @@
 
 
 def per_device(query_weights, tile_terms, tile_blocks, tile_counts, impacts):
-    range_rows = lax.all_gather(query_weights, "doc", axis=1, tiled=True)
+    range_rows = post_state(query_weights)
     queries = range_rows.shape[0]
     tiles, term_block, doc_block = impacts.shape
     owners = lax.axis_size("doc")

time: 313 us -> 308 us (0.984)
  waiting for transfers between devices: 225 us -> 165 us
  starting transfers between devices: 0.08 us -> 54.6 us
    all_gather x1 -> x0, waiting for transfers between devices: 78.3 us -> none  [per_device(): range_rows = lax.all_gather(query_weights, 'doc', axis=1, tiled=True)]
    ppermute x0 -> x15, starting transfers between devices: none -> 54.6 us  [the longest x7 37.3 us: finish_local_data_up(): y1.append(lax.ppermute(y1[-1] if y1 else z_in, row_axis, in_order))]
    ppermute x0 -> x15, waiting for transfers between devices: none -> 17 us  [the longest x8 16.9 us: finish_local_data_up(): p_next.append(lax.ppermute(p_next[-1] if p_next else z_in, row_axis, shelf))]
  transfers between devices with their start and end apart: 3 -> 17, of which waited for: 3 -> 10; matrix products, arithmetic and copies ran while one was open for 0% -> 1% of each run, Pallas kernels for 0% -> 0%
where the time goes in v1:
time: 308 us; the launch traced here: 307 us
  waiting for transfers between devices  165 us (54%)
  starting transfers between devices  54.6 us (18%)
  matrix products  42 us (14%)
  local copies, waits for them, and re-layouts  27.7 us (9%)
  between operations  14.4 us (5%)
    psum x1, waiting for transfers between devices, per_device(): scores = lax.psum(mine, 'term')  75.4 us
    reduce_scatter x1, waiting for transfers between devices, per_device(): lax.psum_scatter(partial_value, 'doc', scatter_dimension=0, tiled=True)  72.6 us
    ppermute x7, starting transfers between devices, finish_local_data_up(): y1.append(lax.ppermute(y1[-1] if y1 else z_in, row_axis, in_order))  37.3 us
    dot_general x4, matrix products, accumulate(): jnp.einsum('ndq,nb->bdq', product, select, precision=lax.Precision.HIGHEST)  31.6 us
    ppermute x8, starting transfers between devices, finish_local_data_up(): p_next.append(lax.ppermute(p_next[-1] if p_next else z_in, row_axis, shelf))  17.3 us
    ppermute x8, waiting for transfers between devices, finish_local_data_up(): p_next.append(lax.ppermute(p_next[-1] if p_next else z_in, row_axis, shelf))  16.9 us
    dot_general x4, matrix products, accumulate(): jnp.einsum('qnk,nkd->ndq', picked, tile_now, preferred_element_type=jnp.f...  10.5 us
    gather x4, local copies, waits for them, and re-layouts, accumulate(): picked = jnp.take(grouped, term_now, axis=1)  8.92 us
  transfers between devices with their start and end apart: 17, of which 10 were waited for; matrix products, arithmetic and copies ran while one was open for 1% of the time, Pallas kernels for 0%

profile of v1, /device:TPU:2, one launch (start us, length us, event | category | flops | bytes accessed | tf_op | source)
XLA Modules:
  0.0 306.9 jit_solution(656643797192978390)
XLA Ops:
  6.5 3.9 %collective-permute-start = (bf16[256,240]{0,1:T(8,128)(2,1)}, bf16[256,240]{0,1:T(8,128)(2,1)S(1)}, u32[]{:S(2)}, u32[]{:S(2)}) collective-permute-start(bf16[256,240]{0,1:T(8,128)(2,1)} %param.7), channel_id=1, source_target_pairs={{0,4},{4,8},{8,12},{12,16},{16,20},{20,24},{24,28},{28,32},{32,36}... | collective-permute-start | bytes 368648 | tf_op jit(solution)/shard_map/ppermute | solution.py:25
  10.5 11.1 %collective-permute-done = bf16[256,240]{0,1:T(8,128)(2,1)S(1)} collective-permute-done((bf16[256,240]{0,1:T(8,128)(2,1)}, bf16[256,240]{0,1:T(8,128)(2,1)S(1)}, u32[]{:S(2)}, u32[]{:S(2)}) %collective-permute-start) | collective-permute-done | bytes 122912 | tf_op jit(solution)/shard_map/ppermute | solution.py:25
  21.6 1.9 collective-permute-start.1
  23.5 5.1 %collective-permute-start.8 = (bf16[256,240]{0,1:T(8,128)(2,1)}, bf16[256,240]{0,1:T(8,128)(2,1)S(1)}, u32[]{:S(2)}, u32[]{:S(2)}) collective-permute-start(bf16[256,240]{0,1:T(8,128)(2,1)} %param.7), channel_id=1, source_target_pairs={{4,0},{8,4},{12,8},{16,12},{20,16},{24,20},{28,24},{32,28},{36,32}... | collective-permute-start | bytes 368648 | tf_op jit(solution)/shard_map/ppermute | solution.py:27
  28.6 0.9 collective-permute-done.1
  29.6 1.9 collective-permute-start.2
  31.5 5.3 %collective-permute-start.9 = (bf16[256,240]{0,1:T(8,128)(2,1)S(1)}, bf16[256,240]{0,1:T(8,128)(2,1)S(1)}, u32[]{:S(2)}, u32[]{:S(2)}) collective-permute-start(bf16[256,240]{0,1:T(8,128)(2,1)S(1)} %collective-permute-done.8), channel_id=1, source_target_pairs={{4,0},{8,4},{12,8},{16,12},{20,16},{24,20},{28,24},{32,28},{36,32}... | collective-permute-start | bytes 368648 | tf_op jit(solution)/shard_map/ppermute | solution.py:27
  36.8 0.7 collective-permute-done.2
  37.5 1.9 collective-permute-start.3
  39.5 5.3 %collective-permute-start.10 = (bf16[256,240]{0,1:T(8,128)(2,1)S(1)}, bf16[256,240]{0,1:T(8,128)(2,1)S(1)}, u32[]{:S(2)}, u32[]{:S(2)}) collective-permute-start(bf16[256,240]{0,1:T(8,128)(2,1)S(1)} %collective-permute-done.9), channel_id=1, source_target_pairs={{4,0},{8,4},{12,8},{16,12},{20,16},{24,20},{28,24},{32,28},{36,32}... | collective-permute-start | bytes 368648 | tf_op jit(solution)/shard_map/ppermute | solution.py:27
  44.8 0.7 collective-permute-done.3
  45.5 1.9 collective-permute-start.4
  47.4 5.3 %collective-permute-start.11 = (bf16[256,240]{0,1:T(8,128)(2,1)S(1)}, bf16[256,240]{0,1:T(8,128)(2,1)S(1)}, u32[]{:S(2)}, u32[]{:S(2)}) collective-permute-start(bf16[256,240]{0,1:T(8,128)(2,1)S(1)} %collective-permute-done.10), channel_id=1, source_target_pairs={{4,0},{8,4},{12,8},{16,12},{20,16},{24,20},{28,24},{32,28},{36,32}... | collective-permute-start | bytes 368648 | tf_op jit(solution)/shard_map/ppermute | solution.py:27
  52.8 0.7 collective-permute-done.4
  53.5 1.9 collective-permute-start.5
  55.4 5.3 %collective-permute-start.12 = (bf16[256,240]{0,1:T(8,128)(2,1)S(1)}, bf16[256,240]{0,1:T(8,128)(2,1)S(1)}, u32[]{:S(2)}, u32[]{:S(2)}) collective-permute-start(bf16[256,240]{0,1:T(8,128)(2,1)S(1)} %collective-permute-done.11), channel_id=1, source_target_pairs={{4,0},{8,4},{12,8},{16,12},{20,16},{24,20},{28,24},{32,28},{36,32}... | collective-permute-start | bytes 368648 | tf_op jit(solution)/shard_map/ppermute | solution.py:27
  60.7 1.5 collective-permute-done.5
  62.3 1.9 collective-permute-start.6
  64.8 5.1 %collective-permute-start.13 = (bf16[256,240]{0,1:T(8,128)(2,1)S(1)}, bf16[256,240]{0,1:T(8,128)(2,1)}, u32[]{:S(2)}, u32[]{:S(2)}) collective-permute-start(bf16[256,240]{0,1:T(8,128)(2,1)S(1)} %collective-permute-done.12), channel_id=1, source_target_pairs={{4,0},{8,4},{12,8},{16,12},{20,16},{24,20},{28,24},{32,28},{36,32}... | collective-permute-start | bytes 368648 | tf_op jit(solution)/shard_map/ppermute | solution.py:27
  70.0 0.9 collective-permute-done.6
  70.9 1.9 collective-permute-start.7
  72.9 5.7 %collective-permute-start.14 = (bf16[256,240]{0,1:T(8,128)(2,1)}, bf16[256,240]{0,1:T(8,128)(2,1)S(1)}, u32[]{:S(2)}, u32[]{:S(2)}) collective-permute-start(bf16[256,240]{0,1:T(8,128)(2,1)} %collective-permute-done.13), channel_id=1, source_target_pairs={{4,0},{8,4},{12,8},{16,12},{20,16},{24,20},{28,24},{32,28},{36,32}... | collective-permute-start | bytes 368648 | tf_op jit(solution)/shard_map/ppermute | solution.py:27
  79.0 0.9 bitcast_dynamic-update-slice_fusion.15
  79.9 0.9 bitcast_dynamic-update-slice_fusion.14
  81.0 0.9 bitcast_dynamic-update-slice_fusion.1
  82.0 1.9 gather_fusion.1
  84.0 62.3 %while.11 = (s32[]{:T(128)}, f32[16,128,256]{2,0,1:T(8,128)}, s32[4]{0:T(128)S(1)}, s32[240]{0:T(256)S(1)}, pred[240]{0:T(512)(128)(4,1)S(1)}, /*index=5*/bf16[2...) while((s32[]{:T(128)}, f32[16,128,256]{2,0,1:T(8,128)}, ...), condition=%wide.region_1.2_spmd.clone, body=%wide.region_0.1_spmd.clone.sunk | while | flops 631180544 | bytes 43587780 | solution.py:72
  84.0 0.6 dynamic_slice.30
  85.5 2.2 gather_fusion
  87.7 2.6 fusion.30
  90.3 7.9 %select_add_fusion.2 = f32[16,128,256]{2,0,1:T(8,128)S(1)} fusion(f32[16,128,256]{2,0,1:T(8,128)S(1)} %copy-done, f32[60,128,256]{2,1,0:T(8,128)S(1)} %fusion.30, pred[]{:T(512)S(6)} %compare.10, s32[60]{0:T(128)S(1)} %dynamic_slice.31, pred[60]{0:T(512)(128)(4,1)S(1)} %dynamic_slice.32), kind=kOutput, calls=%fused_computation.5.clone.1 | convolution fusion | flops 378537856 | bytes 12058925 | tf_op jit(solution)/shard_map/while/body/eval_jaxpr/ndq,nb->bdq/dot_general | solution.py:68
  98.2 1.3 copy-done.1
  101.0 2.2 gather_fusion
  103.3 2.6 fusion.30
  105.9 7.9 %select_add_fusion.2 = f32[16,128,256]{2,0,1:T(8,128)S(1)} fusion(f32[16,128,256]{2,0,1:T(8,128)S(1)} %copy-done, f32[60,128,256]{2,1,0:T(8,128)S(1)} %fusion.30, pred[]{:T(512)S(6)} %compare.10, s32[60]{0:T(128)S(1)} %dynamic_slice.31, pred[60]{0:T(512)(128)(4,1)S(1)} %dynamic_slice.32), kind=kOutput, calls=%fused_computation.5.clone.1 | convolution fusion | flops 378537856 | bytes 12058925 | tf_op jit(solution)/shard_map/while/body/eval_jaxpr/ndq,nb->bdq/dot_general | solution.py:68
  113.8 1.3 copy-done.1
  116.6 2.2 gather_fusion
  118.9 2.6 fusion.30
  121.5 7.9 %select_add_fusion.2 = f32[16,128,256]{2,0,1:T(8,128)S(1)} fusion(f32[16,128,256]{2,0,1:T(8,128)S(1)} %copy-done, f32[60,128,256]{2,1,0:T(8,128)S(1)} %fusion.30, pred[]{:T(512)S(6)} %compare.10, s32[60]{0:T(128)S(1)} %dynamic_slice.31, pred[60]{0:T(512)(128)(4,1)S(1)} %dynamic_slice.32), kind=kOutput, calls=%fused_computation.5.clone.1 | convolution fusion | flops 378537856 | bytes 12058925 | tf_op jit(solution)/shard_map/while/body/eval_jaxpr/ndq,nb->bdq/dot_general | solution.py:68
  129.4 1.3 copy-done.1
  132.2 2.2 gather_fusion
  134.4 2.6 fusion.30
  137.1 7.9 %select_add_fusion.2 = f32[16,128,256]{2,0,1:T(8,128)S(1)} fusion(f32[16,128,256]{2,0,1:T(8,128)S(1)} %copy-done, f32[60,128,256]{2,1,0:T(8,128)S(1)} %fusion.30, pred[]{:T(512)S(6)} %compare.10, s32[60]{0:T(128)S(1)} %dynamic_slice.31, pred[60]{0:T(512)(128)(4,1)S(1)} %dynamic_slice.32), kind=kOutput, calls=%fused_computation.5.clone.1 | convolution fusion | flops 378537856 | bytes 12058925 | tf_op jit(solution)/shard_map/while/body/eval_jaxpr/ndq,nb->bdq/dot_general | solution.py:68
  145.0 1.3 copy-done.1
  146.3 4.1 %copy.8 = f32[16,128,256]{2,1,0:T(8,128)} copy(f32[16,128,256]{2,0,1:T(8,128)} %get-tuple-element.52) | data formatting | bytes 4194304 | tf_op jit(solution)/shard_map/while | solution.py:72
  150.5 72.6 %reduce-scatter.2.cloned.1.call-done = f32[128,256]{1,0:T(8,128)} async-done(((f32[2048,256]{1,0:T(8,128)}), f32[128,256]{1,0:T(8,128)}) %reduce-scatter.2.cloned.1.call-update) | async-done | bytes 131088 | tf_op jit(solution)/shard_map/reduce_scatter | solution.py:74
  223.1 75.4 %all-reduce.2.cloned.1.call-done = f32[128,256]{1,0:T(8,128)} async-done(((f32[128,256]{1,0:T(8,128)}), f32[128,256]{1,0:T(8,128)}) %all-reduce.2.cloned.1.call-update) | async-done | bytes 131088 | tf_op jit(solution)/shard_map/psum | solution.py:75
  298.5 1.6 copy.39
  (69 shorter events, 3.4 us)
Async XLA Ops:
  6.5 74.4 %copy-start.2 = (bf16[256,240]{0,1:T(8,128)(2,1)S(1)}, bf16[256,240]{0,1:T(8,128)(2,1)}, u32[]{:S(2)}) copy-start(bf16[256,240]{0,1:T(8,128)(2,1)} %param.7) | copy-start | bytes 368644
  6.5 216.5 %reduce-scatter.2.cloned.1.call-start = ((), (), s32[]{:S(2)}) async-start(), calls=%async_computation.1 | async-start | bytes 2228224 | tf_op jit(solution)/shard_map/reduce_scatter | solution.py:74
  6.5 15.0 %collective-permute-start = (bf16[256,240]{0,1:T(8,128)(2,1)}, bf16[256,240]{0,1:T(8,128)(2,1)S(1)}, u32[]{:S(2)}, u32[]{:S(2)}) collective-permute-start(bf16[256,240]{0,1:T(8,128)(2,1)} %param.7), channel_id=1, source_target_pairs={{0,4},{4,8},{8,12},{12,16},{16,20},{20,24},{24,28},{28,32},{32,36}... | collective-permute-start | bytes 368648 | tf_op jit(solution)/shard_map/ppermute | solution.py:25
  21.6 8.0 %collective-permute-start.1 = (bf16[256,240]{0,1:T(8,128)(2,1)S(1)}, bf16[256,240]{0,1:T(8,128)(2,1)S(1)}, u32[]{:S(2)}, u32[]{:S(2)}) collective-permute-start(bf16[256,240]{0,1:T(8,128)(2,1)S(1)} %collective-permute-done), channel_id=1, source_target_pairs={{0,4},{4,8},{8,12},{12,16},{16,20},{20,24},{24,28},{28,32},{32,36}... | collective-permute-start | bytes 368648 | tf_op jit(solution)/shard_map/ppermute | solution.py:25
  23.5 8.0 %collective-permute-start.8 = (bf16[256,240]{0,1:T(8,128)(2,1)}, bf16[256,240]{0,1:T(8,128)(2,1)S(1)}, u32[]{:S(2)}, u32[]{:S(2)}) collective-permute-start(bf16[256,240]{0,1:T(8,128)(2,1)} %param.7), channel_id=1, source_target_pairs={{4,0},{8,4},{12,8},{16,12},{20,16},{24,20},{28,24},{32,28},{36,32}... | collective-permute-start | bytes 368648 | tf_op jit(solution)/shard_map/ppermute | solution.py:27
  29.6 8.0 %collective-permute-start.2 = (bf16[256,240]{0,1:T(8,128)(2,1)S(1)}, bf16[256,240]{0,1:T(8,128)(2,1)S(1)}, u32[]{:S(2)}, u32[]{:S(2)}) collective-permute-start(bf16[256,240]{0,1:T(8,128)(2,1)S(1)} %collective-permute-done.1), channel_id=1, source_target_pairs={{0,4},{4,8},{8,12},{12,16},{16,20},{20,24},{24,28},{28,32},{32,36}... | collective-permute-start | bytes 368648 | tf_op jit(solution)/shard_map/ppermute | solution.py:25
  31.5 8.0 %collective-permute-start.9 = (bf16[256,240]{0,1:T(8,128)(2,1)S(1)}, bf16[256,240]{0,1:T(8,128)(2,1)S(1)}, u32[]{:S(2)}, u32[]{:S(2)}) collective-permute-start(bf16[256,240]{0,1:T(8,128)(2,1)S(1)} %collective-permute-done.8), channel_id=1, source_target_pairs={{4,0},{8,4},{12,8},{16,12},{20,16},{24,20},{28,24},{32,28},{36,32}... | collective-permute-start | bytes 368648 | tf_op jit(solution)/shard_map/ppermute | solution.py:27
  37.5 8.0 %collective-permute-start.3 = (bf16[256,240]{0,1:T(8,128)(2,1)S(1)}, bf16[256,240]{0,1:T(8,128)(2,1)S(1)}, u32[]{:S(2)}, u32[]{:S(2)}) collective-permute-start(bf16[256,240]{0,1:T(8,128)(2,1)S(1)} %collective-permute-done.2), channel_id=1, source_target_pairs={{0,4},{4,8},{8,12},{12,16},{16,20},{20,24},{24,28},{28,32},{32,36}... | collective-permute-start | bytes 368648 | tf_op jit(solution)/shard_map/ppermute | solution.py:25
  39.5 8.0 %collective-permute-start.10 = (bf16[256,240]{0,1:T(8,128)(2,1)S(1)}, bf16[256,240]{0,1:T(8,128)(2,1)S(1)}, u32[]{:S(2)}, u32[]{:S(2)}) collective-permute-start(bf16[256,240]{0,1:T(8,128)(2,1)S(1)} %collective-permute-done.9), channel_id=1, source_target_pairs={{4,0},{8,4},{12,8},{16,12},{20,16},{24,20},{28,24},{32,28},{36,32}... | collective-permute-start | bytes 368648 | tf_op jit(solution)/shard_map/ppermute | solution.py:27
  45.5 8.0 %collective-permute-start.4 = (bf16[256,240]{0,1:T(8,128)(2,1)S(1)}, bf16[256,240]{0,1:T(8,128)(2,1)S(1)}, u32[]{:S(2)}, u32[]{:S(2)}) collective-permute-start(bf16[256,240]{0,1:T(8,128)(2,1)S(1)} %collective-permute-done.3), channel_id=1, source_target_pairs={{0,4},{4,8},{8,12},{12,16},{16,20},{20,24},{24,28},{28,32},{32,36}... | collective-permute-start | bytes 368648 | tf_op jit(solution)/shard_map/ppermute | solution.py:25
  47.4 8.0 %collective-permute-start.11 = (bf16[256,240]{0,1:T(8,128)(2,1)S(1)}, bf16[256,240]{0,1:T(8,128)(2,1)S(1)}, u32[]{:S(2)}, u32[]{:S(2)}) collective-permute-start(bf16[256,240]{0,1:T(8,128)(2,1)S(1)} %collective-permute-done.10), channel_id=1, source_target_pairs={{4,0},{8,4},{12,8},{16,12},{20,16},{24,20},{28,24},{32,28},{36,32}... | collective-permute-start | bytes 368648 | tf_op jit(solution)/shard_map/ppermute | solution.py:27
  53.5 8.8 %collective-permute-start.5 = (bf16[256,240]{0,1:T(8,128)(2,1)S(1)}, bf16[256,240]{0,1:T(8,128)(2,1)S(1)}, u32[]{:S(2)}, u32[]{:S(2)}) collective-permute-start(bf16[256,240]{0,1:T(8,128)(2,1)S(1)} %collective-permute-done.4), channel_id=1, source_target_pairs={{0,4},{4,8},{8,12},{12,16},{16,20},{20,24},{24,28},{28,32},{32,36}... | collective-permute-start | bytes 368648 | tf_op jit(solution)/shard_map/ppermute | solution.py:25
  55.4 9.4 %collective-permute-start.12 = (bf16[256,240]{0,1:T(8,128)(2,1)S(1)}, bf16[256,240]{0,1:T(8,128)(2,1)S(1)}, u32[]{:S(2)}, u32[]{:S(2)}) collective-permute-start(bf16[256,240]{0,1:T(8,128)(2,1)S(1)} %collective-permute-done.11), channel_id=1, source_target_pairs={{4,0},{8,4},{12,8},{16,12},{20,16},{24,20},{28,24},{32,28},{36,32}... | collective-permute-start | bytes 368648 | tf_op jit(solution)/shard_map/ppermute | solution.py:27
  62.3 8.7 %collective-permute-start.6 = (bf16[256,240]{0,1:T(8,128)(2,1)S(1)}, bf16[256,240]{0,1:T(8,128)(2,1)S(1)}, u32[]{:S(2)}, u32[]{:S(2)}) collective-permute-start(bf16[256,240]{0,1:T(8,128)(2,1)S(1)} %collective-permute-done.5), channel_id=1, source_target_pairs={{0,4},{4,8},{8,12},{12,16},{16,20},{20,24},{24,28},{28,32},{32,36}... | collective-permute-start | bytes 368648 | tf_op jit(solution)/shard_map/ppermute | solution.py:25
  64.8 8.1 %collective-permute-start.13 = (bf16[256,240]{0,1:T(8,128)(2,1)S(1)}, bf16[256,240]{0,1:T(8,128)(2,1)}, u32[]{:S(2)}, u32[]{:S(2)}) collective-permute-start(bf16[256,240]{0,1:T(8,128)(2,1)S(1)} %collective-permute-done.12), channel_id=1, source_target_pairs={{4,0},{8,4},{12,8},{16,12},{20,16},{24,20},{28,24},{32,28},{36,32}... | collective-permute-start | bytes 368648 | tf_op jit(solution)/shard_map/ppermute | solution.py:27
  70.9 7.7 %copy-start.3 = (bf16[256,240]{0,1:T(8,128)(2,1)}, bf16[256,240]{0,1:T(8,128)(2,1)S(1)}, u32[]{:S(2)}) copy-start(bf16[256,240]{0,1:T(8,128)(2,1)S(1)} %collective-permute-done.6) | copy-start | bytes 368644
  70.9 8.1 %collective-permute-start.7 = (bf16[256,240]{0,1:T(8,128)(2,1)S(1)}, bf16[256,240]{0,1:T(8,128)(2,1)}, u32[]{:S(2)}, u32[]{:S(2)}) collective-permute-start(bf16[256,240]{0,1:T(8,128)(2,1)S(1)} %collective-permute-done.6), channel_id=1, source_target_pairs={{0,4},{4,8},{8,12},{12,16},{16,20},{20,24},{24,28},{28,32},{32,36}... | collective-permute-start | bytes 368648 | tf_op jit(solution)/shard_map/ppermute | solution.py:25
  72.9 9.1 %collective-permute-start.14 = (bf16[256,240]{0,1:T(8,128)(2,1)}, bf16[256,240]{0,1:T(8,128)(2,1)S(1)}, u32[]{:S(2)}, u32[]{:S(2)}) collective-permute-start(bf16[256,240]{0,1:T(8,128)(2,1)} %collective-permute-done.13), channel_id=1, source_target_pairs={{4,0},{8,4},{12,8},{16,12},{20,16},{24,20},{28,24},{32,28},{36,32}... | collective-permute-start | bytes 368648 | tf_op jit(solution)/shard_map/ppermute | solution.py:27
  82.0 2.0 copy-start.4
  82.0 2.0 copy-start.5
  87.7 2.6 copy-start
  98.2 1.3 copy-start.1
  103.3 2.6 copy-start
  113.8 1.3 copy-start.1
  118.9 2.6 copy-start
  129.4 1.3 copy-start.1
  134.4 2.6 copy-start
  145.0 1.3 copy-start.1
  150.4 148.1 %all-reduce.2.cloned.1.call-start = ((), (), s32[]{:S(2)}) async-start(), calls=%async_computation.2 | async-start | bytes 262144 | tf_op jit(solution)/shard_map/psum | solution.py:75
Sparse Core Ops, SparseCore 0:
  150.5 72.4 reduce-scatter.1
  225.3 73.0 all-reduce.1
